TPU v7x, 32 devices: a whole 2x2x4 slice. The times are simulated.
32 devices in a mesh: segment: 4 (over y, x), ctx: 8 (over z, core).
Axes of the slice: x: 2, y: 2, z: 4, core: 2. Of those that a mesh axis runs over, the one named last changes fastest.
Arguments:
- segment_input: bfloat16 [4, 1024, 2048], P('segment', 'ctx'), may hold values from -6 to 6
- views: bfloat16 [4, 16, 128, 384], P('segment'), may hold values from -0.5 to 0.5
- gate_vec: float32 [4, 16, 128], P('segment'), may hold values from -0.9 to 0.9
- base_rate: float32 [4, 16], P('segment'), may hold values from 0.05 to 1.5
- norm_gain: float32 [4, 16, 128], P('segment'), may hold values from 0.5 to 1.5
- init_weight: float32 [4, 16, 128, 128], P('segment'), may hold values from -0.5 to 0.5
- out_grad: bfloat16 [4, 1024, 2048], P('segment', 'ctx'), may hold values from -6 to 6
Outputs:
- next_input: bfloat16 [4, 1024, 2048], P('segment', 'ctx')
- view_grad: float32 [4, 16, 128, 384], P('segment', 'ctx')
- gate_grad: float32 [4, 16, 128], P('segment', 'ctx')
- rate_grad: float32 [4, 16], P('segment', 'ctx')
- gain_grad: float32 [4, 16, 128], P('segment', 'ctx')
- init_grad: float32 [4, 16, 128, 128], P('segment', 'ctx')
- input_grad: bfloat16 [4, 1024, 2048], P('segment', 'ctx')
All inputs are finite; a program needn't handle non-finite values.
Results may differ from a plain program's by a relative error of at most 0.001.
Values may be sent and summed in bfloat16 or wider, within the bound.
A program may use at most 128 MiB of HBM per device.

v0:
```python
import functools

import jax
import jax.numpy as jnp
from jax import lax
from jax.experimental import pallas as pl
from jax.experimental.pallas import tpu as pltpu
from jax.sharding import PartitionSpec as P

MB = 16
F32 = jnp.float32
BF16 = jnp.bfloat16
NN = (((1,), (0,)), ((), ()))
NT = (((1,), (1,)), ((), ()))
TN = (((0,), (0,)), ((), ()))


def dot(left, right, dims):
    return lax.dot_general(left, right, dims, preferred_element_type=F32)


def split(value):
    high = value.astype(BF16)
    low = (value - high.astype(F32)).astype(BF16)
    return high, low


def cat(parts, axis):
    return jnp.concatenate(parts, axis=axis)


def stack(left, right, axis):
    return cat([left[0], right[0]], axis), cat([left[1], right[1]], axis)


def product(left, right, dims):
    left_axis, right_axis = dims[0][0][0], dims[0][1][0]
    left_both = cat(left, left_axis)
    wide = cat(right, 1 - right_axis)
    result = dot(left_both, cat([wide, wide], right_axis), dims)
    columns = result.shape[1] // 2
    return result[:, :columns] + result[:, columns:]


def row_mean(value):
    return jnp.mean(value, axis=-1, keepdims=True)


def positions(size):
    rows = lax.broadcasted_iota(jnp.int32, (size, size), 0)
    columns = lax.broadcasted_iota(jnp.int32, (size, size), 1)
    return rows, columns


def block_inverse(strict, size):
    rows, columns = positions(size)
    width = MB
    eye = jnp.where(rows == columns, 1.0, 0.0).astype(F32)
    inverse = eye
    while width < size:
        same = (rows // (2 * width)) == (columns // (2 * width))
        below = (rows // width) > (columns // width)
        corner = jnp.where(same & below, strict, 0.0)
        if width == MB:
            inverse = eye - corner
        else:
            pair = split(inverse)
            inverse = inverse - product(split(product(pair, split(corner), NN)), pair, NN)
        width *= 2
    return inverse


def kernel(
    count, heads, size, width,
    x_ref, og_ref, views_ref, gate_ref, rate_ref, gain_ref, init_ref,
    out_ref, vgrad_ref, ggrad_ref, rgrad_ref, ngrad_ref, igrad_ref, dx_ref,
    view_buf, init_buf, qs, ks, krs, qes, as_, ss, ts, fs, rs, dzs, ws, gs,
    kf, bs, sbs, os_, v0s, ls, invs, sigs, load_sem,
):
    me = lax.axis_index("ctx")
    first_head = me * heads
    loads = [
        pltpu.make_async_copy(views_ref.at[0, pl.ds(first_head, heads)], view_buf, load_sem.at[0]),
        pltpu.make_async_copy(init_ref.at[0, pl.ds(first_head, heads)], init_buf, load_sem.at[1]),
    ]
    for load in loads:
        load.start()
    for load in loads:
        load.wait()
    scale = 1.0 / (MB * width)

    def columns_of(h):
        return slice(h * width, (h + 1) * width)

    def gate_of(h):
        return gate_ref[0, pl.ds(first_head + h, 1), :]

    def gain_of(h):
        return gain_ref[0, pl.ds(first_head + h, 1), :]

    def base_of(h):
        lane = lax.broadcasted_iota(jnp.int32, rate_ref.shape, 1)
        return jnp.sum(jnp.where(lane == first_head + h, rate_ref[...], 0.0), axis=1, keepdims=True)

    def put(ref, c, h, pair):
        ref[c, h, 0] = pair[0]
        ref[c, h, 1] = pair[1]

    def get(ref, c, h):
        return ref[c, h, 0], ref[c, h, 1]

    def masks():
        rows, columns = positions(size)
        return rows >= columns, (rows // MB) > (columns // MB)

    def prepare(c, h):
        x = x_ref[c, :, columns_of(h)]
        packed = dot(x, view_buf[h], NN)
        q = packed[:, :width]
        raw = packed[:, width : 2 * width]
        inv = lax.rsqrt(row_mean(raw * raw) + 1e-06)
        k = raw * inv
        y = packed[:, 2 * width :] - k
        logit = jnp.sum(x.astype(F32) * gate_of(h), axis=-1, keepdims=True)
        sig = jax.nn.sigmoid(logit)
        kr = k * (base_of(h) * sig * scale)
        k2, q2, kr2 = split(k), split(q), split(kr)
        causal, before = masks()
        grams = product(stack(k2, q2, 0), kr2, NT)
        inverse = block_inverse(jnp.where(before, grams[:size], 0.0), size)
        scores = split(jnp.where(causal, grams[size:], 0.0))
        t2 = split(inverse)
        ab = product(t2, stack(k2, split(y), 1), NN)
        ab2 = split(ab)
        sab = product(scores, ab2, NN)
        fo = product(kr2, ab2, TN)
        put(qs, c, h, q2)
        put(ks, c, h, k2)
        put(krs, c, h, kr2)
        put(qes, c, h, split(q - sab[:, :width]))
        put(as_, c, h, (ab2[0][:, :width], ab2[1][:, :width]))
        put(ss, c, h, scores)
        put(ts, c, h, t2)
        put(fs, c, h, split(fo[:, :width]))
        kf[c, h] = k
        bs[c, h] = ab[:, width:]
        sbs[c, h] = sab[:, width:]
        os_[c, h] = fo[:, width:]
        invs[c, h] = inv
        sigs[c, h] = sig

    def advance(c, h):
        w2 = split(init_buf[h])
        put(ws, c, h, w2)
        init_buf[h] = init_buf[h] - product(get(fs, c, h), w2, NN) + os_[c, h]

    def outputs(c, h):
        cols = columns_of(h)
        qe = get(qes, c, h)
        moved = product(stack(qe, get(as_, c, h), 0), get(ws, c, h), NN)
        z = moved[:size] + sbs[c, h]
        put(rs, c, h, split(moved[size:] - bs[c, h]))
        centred = z - row_mean(z)
        rstd = lax.rsqrt(row_mean(centred * centred) + 1e-05)
        normed = centred * rstd
        gain = gain_of(h)
        out_ref[c, :, cols] = (x_ref[c, :, cols].astype(F32) + gain * normed).astype(BF16)
        dout = og_ref[c, :, cols].astype(F32)
        ngrad_ref[0, h : h + 1, :] += jnp.sum(dout * normed, axis=0, keepdims=True)
        dn = dout * gain
        dz = rstd * (dn - row_mean(dn) - normed * row_mean(dn * normed))
        dz2 = split(dz)
        put(dzs, c, h, dz2)
        back = product(stack(qe, get(ss, c, h), 1), dz2, TN)
        ls[c, h] = back[:width]
        v0s[c, h] = back[width:]

    def retreat(c, h):
        g = igrad_ref[0, h]
        g2 = split(g)
        put(gs, c, h, g2)
        igrad_ref[0, h] = g - product(get(fs, c, h), g2, TN) + ls[c, h]

    def gradients(c, h):
        cols = columns_of(h)
        g2, kr2, w2, r2, dz2 = get(gs, c, h), get(krs, c, h), get(ws, c, h), get(rs, c, h), get(dzs, c, h)
        v = v0s[c, h] + product(kr2, g2, NN)
        du = -product(get(ts, c, h), split(v), TN)
        both = stack(dz2, split(du), 0)
        causal, before = masks()
        inner = product(both, r2, NT)
        dscores = jnp.where(causal, -inner[:size], 0.0)
        dstrict = jnp.where(before, -inner[size:], 0.0)
        d2 = stack(split(dscores), split(dstrict), 0)
        dqk = product(both, w2, NT) + product(d2, kr2, NN)
        dkr = product(d2, stack(get(qs, c, h), get(ks, c, h), 0), TN) - product(r2, g2, NT)
        sig, inv, k, base = sigs[c, h], invs[c, h], kf[c, h], base_of(h)
        rate_factor = sig * scale
        dk = dqk[size:] + (base * rate_factor) * dkr + du
        draw = inv * (dk - k * row_mean(dk * k))
        drate = jnp.sum(dkr * k, axis=-1, keepdims=True) * rate_factor
        rgrad_ref[:, h : h + 1] += jnp.sum(drate, axis=0, keepdims=True)
        dlogit = drate * base * (1.0 - sig)
        x = x_ref[c, :, cols]
        ggrad_ref[0, h : h + 1, :] += jnp.sum(dlogit * x.astype(F32), axis=0, keepdims=True)
        packed = split(cat([dqk[:size], draw, -du], 1))
        vgrad_ref[0, h] += dot(cat([x, x], 0), cat(packed, 0), TN)
        views = view_buf[h]
        dx = dot(packed[0], views, NT) + dot(packed[1], views, NT)
        dx = dx + og_ref[c, :, cols].astype(F32) + dlogit * gate_of(h)
        dx_ref[c, :, cols] = dx.astype(BF16)

    for ref in (vgrad_ref, ggrad_ref, rgrad_ref, ngrad_ref, igrad_ref):
        ref[...] = jnp.zeros_like(ref)

    all_heads = range(heads)

    def forward(c, carry):
        for h in all_heads:
            prepare(c, h)
        for h in all_heads:
            advance(c, h)
        for h in all_heads:
            outputs(c, h)
        return carry

    lax.fori_loop(0, count, forward, 0)

    def backward(step, carry):
        c = count - 1 - step
        for h in all_heads:
            retreat(c, h)
        for h in all_heads:
            gradients(c, h)
        return carry

    lax.fori_loop(0, count, backward, 0)


def per_device(segment_input, views, gate_vec, base_rate, norm_gain, init_weight, out_grad):
    count = lax.axis_size("ctx")
    size, features = segment_input.shape[1:]
    total, width = gate_vec.shape[1:]
    heads = total // count
    local = heads * width

    def spread(value):
        parts = value[0].reshape(size, count, local).swapaxes(0, 1)
        return lax.all_to_all(parts, "ctx", 0, 0, tiled=True)

    def collect(value, steps):
        moved = lax.all_to_all(value, "ctx", 0, 0, tiled=True)
        number = lax.axis_size("segment")
        pairs = [(source, (source + steps) % number) for source in range(number)]
        moved = lax.ppermute(moved, "segment", pairs)
        return moved.swapaxes(0, 1).reshape(1, size, features)

    def shaped(shape, kind):
        return jax.ShapeDtypeStruct(shape, kind)

    vmem = pl.BlockSpec(memory_space=pltpu.VMEM)
    hbm = pl.BlockSpec(memory_space=pl.ANY)

    def pairs(rows, columns):
        return pltpu.VMEM((count, heads, 2, rows, columns), BF16)

    def floats(rows, columns):
        return pltpu.VMEM((count, heads, rows, columns), F32)

    result = pl.pallas_call(
        functools.partial(kernel, count, heads, size, width),
        out_shape=(
            shaped((count, size, local), BF16),
            shaped((1, heads, width, 3 * width), F32),
            shaped((1, heads, width), F32),
            shaped((1, heads), F32),
            shaped((1, heads, width), F32),
            shaped((1, heads, width, width), F32),
            shaped((count, size, local), BF16),
        ),
        in_specs=[vmem, vmem, hbm, vmem, vmem, vmem, hbm],
        out_specs=(vmem,) * 7,
        scratch_shapes=[
            pltpu.VMEM((heads, width, 3 * width), BF16),
            pltpu.VMEM((heads, width, width), F32),
            pairs(size, width), pairs(size, width), pairs(size, width), pairs(size, width), pairs(size, width),
            pairs(size, size), pairs(size, size), pairs(width, width),
            pairs(size, width), pairs(size, width), pairs(width, width), pairs(width, width),
            floats(size, width), floats(size, width), floats(size, width), floats(width, width),
            floats(size, width), floats(width, width),
            floats(size, 1), floats(size, 1),
            pltpu.SemaphoreType.DMA((2,)),
        ],
        compiler_params=pltpu.CompilerParams(vmem_limit_bytes=56 * 1024 * 1024),
    )(
        spread(segment_input), spread(out_grad), views, gate_vec, base_rate, norm_gain, init_weight
    )
    out, vgrad, ggrad, rgrad, ngrad, igrad, dx = result
    return (collect(out, 1), vgrad, ggrad, rgrad, ngrad, igrad, collect(dx, -1))


def solution(mesh):
    return jax.shard_map(
        per_device,
        mesh=mesh,
        in_specs=(
            P("segment", "ctx", None),
            P("segment", None, None, None),
            P("segment", None, None),
            P("segment", None),
            P("segment", None, None),
            P("segment", None, None, None),
            P("segment", "ctx", None),
        ),
        out_specs=(
            P("segment", "ctx", None),
            P("segment", "ctx", None, None),
            P("segment", "ctx", None),
            P("segment", "ctx"),
            P("segment", "ctx", None),
            P("segment", "ctx", None, None),
            P("segment", "ctx", None),
        ),
        check_vma=False,
    )
```

profile of v0, /device:TPU:0, one launch (start us, length us, event | category | flops | bytes accessed | tf_op | source)
XLA Modules:
  0.0 141.4 jit_solution(4211815248723311427)
XLA Ops:
  0.6 0.0 copy-start.1
  0.6 1.4 copy.14
  2.0 1.0 copy.15
  3.0 6.3 %all-to-all-start = ((bf16[8,128,256]{2,1,0:T(8,128)(2,1)}), bf16[8,128,256]{2,1,0:T(8,128)(2,1)S(1)}, u32[]{:S(2)}, u32[]{:S(2)}) async-start(bf16[8,128,256]{2,1,0:T(8,128)(2,1)} %bitcast.1), calls=%async_computation | async-start | bytes 1048576 | tf_op jit(solution)/shard_map/all_to_all | solution.py:249
  9.4 0.0 copy-done.1
  9.4 0.3 copy.16
  9.6 0.2 copy.17
  9.9 14.9 %all-to-all-done.x_ref = bf16[8,128,256]{2,1,0:T(8,128)(2,1)S(1)} async-done(((bf16[8,128,256]{2,1,0:T(8,128)(2,1)}), bf16[8,128,256]{2,1,0:T(8,128)(2,1)S(1)}, u32[]{:S(2)}, u32[]{:S(2)}) %all-to-all-start) | async-done | bytes 524320 | tf_op jit(solution)/shard_map/all_to_all | solution.py:249
  24.7 0.0 copy-start
  24.7 18.4 %all_to_all.20.og_ref = bf16[8,128,256]{2,1,0:T(8,128)(2,1)} all-to-all(bf16[8,128,256]{2,1,0:T(8,128)(2,1)S(1)} %bitcast.8), channel_id=1, replica_groups=mesh['segment'=4,'ctx'=8] {'ctx'}, dimensions={0} | all-to-all | bytes 1048576 | tf_op jit(solution)/shard_map/all_to_all | solution.py:249
  43.2 0.0 copy-done
  43.2 45.0 %shard_map.126 = (bf16[8,128,256]{2,1,0:T(8,128)(2,1)}, f32[1,2,128,384]{3,2,1,0:T(8,128)}, f32[1,2,128]{2,1,0:T(2,128)}, f32[1,2]{1,0:T(1,128)}, f32[1,2,128]{2...) custom-call(bf16[8,128,256]{2,1,0:T(8,128)(2,1)} %copy-done, ...), custom_call_target="tpu_custom_call" | custom-call | tf_op jit(solution)/shard_map/pallas_call | solution.py:270
  88.2 18.8 %all_to_all.21 = bf16[8,128,256]{2,1,0:T(8,128)(2,1)S(1)} all-to-all(bf16[8,128,256]{2,1,0:T(8,128)(2,1)} %get-tuple-element.20), channel_id=1, replica_groups=mesh['segment'=4,'ctx'=8] {'ctx'}, dimensions={0} | all-to-all | bytes 1048576 | tf_op jit(solution)/shard_map/all_to_all | solution.py:252
  107.0 3.5 %all-to-all-start.2 = ((bf16[8,128,256]{2,1,0:T(8,128)(2,1)}), bf16[8,128,256]{2,1,0:T(8,128)(2,1)S(1)}, u32[]{:S(2)}, u32[]{:S(2)}) async-start(bf16[8,128,256]{2,1,0:T(8,128)(2,1)} %get-tuple-element.14), calls=%async_computation.2 | async-start | bytes 1048576 | tf_op jit(solution)/shard_map/all_to_all | solution.py:252
  110.5 2.5 %collective-permute-start.1 = (bf16[8,128,256]{2,1,0:T(8,128)(2,1)S(1)}, bf16[8,128,256]{2,1,0:T(8,128)(2,1)S(1)}, u32[]{:S(2)}, u32[]{:S(2)}) collective-permute-start(bf16[8,128,256]{2,1,0:T(8,128)(2,1)S(1)} %all_to_all.21), channel_id=1, source_target_pairs={{0,24},{8,0},{16,8},{24,16},{1,25},{9,1},{17,9},{25,17},{2,26},{10... | collective-permute-start | bytes 1572872 | tf_op jit(solution)/shard_map/ppermute | solution.py:255
  113.0 12.8 %all-to-all-done.2 = bf16[8,128,256]{2,1,0:T(8,128)(2,1)S(1)} async-done(((bf16[8,128,256]{2,1,0:T(8,128)(2,1)}), bf16[8,128,256]{2,1,0:T(8,128)(2,1)S(1)}, u32[]{:S(2)}, u32[]{:S(2)}) %all-to-all-start.2) | async-done | bytes 524320 | tf_op jit(solution)/shard_map/all_to_all | solution.py:252
  125.8 1.5 %collective-permute-start = (bf16[8,128,256]{2,1,0:T(8,128)(2,1)S(1)}, bf16[8,128,256]{2,1,0:T(8,128)(2,1)S(1)}, u32[]{:S(2)}, u32[]{:S(2)}) collective-permute-start(bf16[8,128,256]{2,1,0:T(8,128)(2,1)S(1)} %all-to-all-done.2), channel_id=1, source_target_pairs={{0,8},{8,16},{16,24},{24,0},{1,9},{9,17},{17,25},{25,1},{2,10},{10... | collective-permute-start | bytes 1572872 | tf_op jit(solution)/shard_map/ppermute | solution.py:255
  127.3 0.0 collective-permute-done.1
  127.3 0.3 copy.19
  127.5 1.0 copy.21
  128.5 11.6 %collective-permute-done = bf16[8,128,256]{2,1,0:T(8,128)(2,1)S(1)} collective-permute-done((bf16[8,128,256]{2,1,0:T(8,128)(2,1)S(1)}, bf16[8,128,256]{2,1,0:T(8,128)(2,1)S(1)}, u32[]{:S(2)}, u32[]{:S(2)}) %collective-permute-start) | collective-permute-done | bytes 524320 | tf_op jit(solution)/shard_map/ppermute | solution.py:255
  140.1 0.3 copy.18
  140.4 1.0 copy.20
Async XLA Ops:
  0.6 8.7 %copy-start.1 = (bf16[1,128,2048]{2,1,0:T(8,128)(2,1)S(1)}, bf16[1,128,2048]{2,1,0:T(8,128)(2,1)}, u32[]{:S(2)}) copy-start(bf16[1,128,2048]{2,1,0:T(8,128)(2,1)} %param.13) | copy-start | bytes 1572868
  3.0 21.7 %all-to-all-start = ((bf16[8,128,256]{2,1,0:T(8,128)(2,1)}), bf16[8,128,256]{2,1,0:T(8,128)(2,1)S(1)}, u32[]{:S(2)}, u32[]{:S(2)}) async-start(bf16[8,128,256]{2,1,0:T(8,128)(2,1)} %bitcast.1), calls=%async_computation | async-start | bytes 1048576 | tf_op jit(solution)/shard_map/all_to_all | solution.py:249
  24.7 18.4 %copy-start = (bf16[8,128,256]{2,1,0:T(8,128)(2,1)}, bf16[8,128,256]{2,1,0:T(8,128)(2,1)S(1)}, u32[]{:S(2)}) copy-start(bf16[8,128,256]{2,1,0:T(8,128)(2,1)S(1)} %all-to-all-done.x_ref) | copy-start | bytes 1572868
  107.0 18.8 %all-to-all-start.2 = ((bf16[8,128,256]{2,1,0:T(8,128)(2,1)}), bf16[8,128,256]{2,1,0:T(8,128)(2,1)S(1)}, u32[]{:S(2)}, u32[]{:S(2)}) async-start(bf16[8,128,256]{2,1,0:T(8,128)(2,1)} %get-tuple-element.14), calls=%async_computation.2 | async-start | bytes 1048576 | tf_op jit(solution)/shard_map/all_to_all | solution.py:252
  110.5 16.8 %collective-permute-start.1 = (bf16[8,128,256]{2,1,0:T(8,128)(2,1)S(1)}, bf16[8,128,256]{2,1,0:T(8,128)(2,1)S(1)}, u32[]{:S(2)}, u32[]{:S(2)}) collective-permute-start(bf16[8,128,256]{2,1,0:T(8,128)(2,1)S(1)} %all_to_all.21), channel_id=1, source_target_pairs={{0,24},{8,0},{16,8},{24,16},{1,25},{9,1},{17,9},{25,17},{2,26},{10... | collective-permute-start | bytes 1572872 | tf_op jit(solution)/shard_map/ppermute | solution.py:255
  125.8 14.4 %collective-permute-start = (bf16[8,128,256]{2,1,0:T(8,128)(2,1)S(1)}, bf16[8,128,256]{2,1,0:T(8,128)(2,1)S(1)}, u32[]{:S(2)}, u32[]{:S(2)}) collective-permute-start(bf16[8,128,256]{2,1,0:T(8,128)(2,1)S(1)} %all-to-all-done.2), channel_id=1, source_target_pairs={{0,8},{8,16},{16,24},{24,0},{1,9},{9,17},{17,25},{25,1},{2,10},{10... | collective-permute-start | bytes 1572872 | tf_op jit(solution)/shard_map/ppermute | solution.py:255
where the time goes:
time: 142 us; the launch traced here: 141 us
  Pallas kernels  45 us (32%)
  waiting for transfers between devices  39.2 us (28%)
  blocking collectives  37.2 us (26%)
  starting transfers between devices  13.8 us (10%)
  local copies, waits for them, and re-layouts  5.44 us (4%)
    pallas_call x1, Pallas kernels, per_device(): pl.pallas_call(functools.partial(kernel, count, heads, size, width), out_...  45 us
    all_to_all x1, blocking collectives, collect(): moved = lax.all_to_all(value, 'ctx', 0, 0, tiled=True)  18.8 us
    all_to_all x1, blocking collectives, spread(): return lax.all_to_all(parts, 'ctx', 0, 0, tiled=True)  18.4 us
    all_to_all x1, waiting for transfers between devices, spread(): return lax.all_to_all(parts, 'ctx', 0, 0, tiled=True)  14.9 us
    all_to_all x1, waiting for transfers between devices, collect(): moved = lax.all_to_all(value, 'ctx', 0, 0, tiled=True)  12.8 us
    ppermute x2, waiting for transfers between devices, collect(): moved = lax.ppermute(moved, 'segment', pairs)  11.6 us
    all_to_all x1, starting transfers between devices, spread(): return lax.all_to_all(parts, 'ctx', 0, 0, tiled=True)  6.33 us
    ppermute x2, starting transfers between devices, collect(): moved = lax.ppermute(moved, 'segment', pairs)  3.99 us
  transfers between devices with their start and end apart: 4, of which 3 were waited for; matrix products, arithmetic and copies ran while one was open for 1% of the time, Pallas kernels for 0%

commit v1 on v0

--- a/solution.py
+++ b/solution.py
@@ -10,6 +10,7 @@
 MB = 16
 F32 = jnp.float32
 BF16 = jnp.bfloat16
+MESH = pl.DeviceIdType.MESH
 NN = (((1,), (0,)), ((), ()))
 NT = (((1,), (1,)), ((), ()))
 TN = (((0,), (0,)), ((), ()))
@@ -71,21 +72,81 @@
 
 
 def kernel(
-    count, heads, size, width,
+    count, sections, heads, size, width,
     x_ref, og_ref, views_ref, gate_ref, rate_ref, gain_ref, init_ref,
-    out_ref, vgrad_ref, ggrad_ref, rgrad_ref, ngrad_ref, igrad_ref, dx_ref,
-    view_buf, init_buf, qs, ks, krs, qes, as_, ss, ts, fs, rs, dzs, ws, gs,
-    kf, bs, sbs, os_, v0s, ls, invs, sigs, load_sem,
+    next_ref, vgrad_ref, ggrad_ref, rgrad_ref, ngrad_ref, igrad_ref, prev_ref,
+    view_buf, init_buf, x_buf, og_buf, out_buf, dx_buf,
+    qs, ks, krs, qes, as_, ss, ts, fs, rs, dzs, ws,
+    kf, bs, sbs, os_, v0s, ls, invs, sigs,
+    load_sem, x_send, x_recv, og_send, og_recv, out_send, out_recv, dx_send, dx_recv,
 ):
     me = lax.axis_index("ctx")
+    section = lax.axis_index("segment")
+    after = (section + 1) % sections
+    before_me = (section + sections - 1) % sections
     first_head = me * heads
+    local = heads * width
+
+    def partner(step):
+        if count & (count - 1):
+            return (me + step) % count
+        total, bit = 0, 1
+        while bit < count:
+            total = total + (((me // bit) + (step // bit)) % 2) * bit
+            bit *= 2
+        return total
+
+    def own_columns(owner):
+        return pl.ds(pl.multiple_of(owner * local, local), local)
+
     loads = [
         pltpu.make_async_copy(views_ref.at[0, pl.ds(first_head, heads)], view_buf, load_sem.at[0]),
         pltpu.make_async_copy(init_ref.at[0, pl.ds(first_head, heads)], init_buf, load_sem.at[1]),
+        pltpu.make_async_copy(x_ref.at[0, :, own_columns(me)], x_buf.at[me], x_recv.at[me]),
+        pltpu.make_async_copy(og_ref.at[0, :, own_columns(me)], og_buf.at[me], og_recv.at[me]),
     ]
     for load in loads:
         load.start()
-    for load in loads:
+
+    barrier = pltpu.get_barrier_semaphore()
+    for step in range(1, count):
+        pl.semaphore_signal(barrier, inc=1, device_id=(section, partner(step)), device_id_type=MESH)
+    for step in range(count):
+        pl.semaphore_signal(barrier, inc=1, device_id=(after, partner(step)), device_id_type=MESH)
+        pl.semaphore_signal(barrier, inc=1, device_id=(before_me, partner(step)), device_id_type=MESH)
+    pl.semaphore_wait(barrier, 3 * count - 1)
+
+    def spread(source, target, send, receive, step):
+        owner = partner(step)
+        return pltpu.make_async_remote_copy(
+            src_ref=source.at[0, :, own_columns(owner)],
+            dst_ref=target.at[me],
+            send_sem=send.at[step],
+            recv_sem=receive.at[me],
+            device_id=(section, owner),
+            device_id_type=MESH,
+        )
+
+    def arrived(target, receive, c):
+        pltpu.make_async_copy(target.at[c], target.at[c], receive.at[c]).wait()
+
+    def collect(source, target, send, receive, c, to):
+        return pltpu.make_async_remote_copy(
+            src_ref=source.at[c],
+            dst_ref=target.at[0, :, own_columns(me)],
+            send_sem=send.at[c],
+            recv_sem=receive.at[me],
+            device_id=(to, c),
+            device_id_type=MESH,
+        )
+
+    def collected(target, receive, c):
+        place = target.at[0, :, own_columns(c)]
+        pltpu.make_async_copy(place, place, receive.at[c]).wait()
+
+    for step in range(1, count):
+        spread(x_ref, x_buf, x_send, x_recv, step).start()
+    for load in loads[:2]:
         load.wait()
     scale = 1.0 / (MB * width)
 
@@ -114,7 +175,7 @@
         return rows >= columns, (rows // MB) > (columns // MB)
 
     def prepare(c, h):
-        x = x_ref[c, :, columns_of(h)]
+        x = x_buf[c, :, columns_of(h)]
         packed = dot(x, view_buf[h], NN)
         q = packed[:, :width]
         raw = packed[:, width : 2 * width]
@@ -149,23 +210,21 @@
         invs[c, h] = inv
         sigs[c, h] = sig
 
-    def advance(c, h):
-        w2 = split(init_buf[h])
-        put(ws, c, h, w2)
+    def advance(c, h, w2):
         init_buf[h] = init_buf[h] - product(get(fs, c, h), w2, NN) + os_[c, h]
 
-    def outputs(c, h):
+    def outputs(c, h, w2):
         cols = columns_of(h)
         qe = get(qes, c, h)
-        moved = product(stack(qe, get(as_, c, h), 0), get(ws, c, h), NN)
+        moved = product(stack(qe, get(as_, c, h), 0), w2, NN)
         z = moved[:size] + sbs[c, h]
         put(rs, c, h, split(moved[size:] - bs[c, h]))
         centred = z - row_mean(z)
         rstd = lax.rsqrt(row_mean(centred * centred) + 1e-05)
         normed = centred * rstd
         gain = gain_of(h)
-        out_ref[c, :, cols] = (x_ref[c, :, cols].astype(F32) + gain * normed).astype(BF16)
-        dout = og_ref[c, :, cols].astype(F32)
+        out_buf[c, :, cols] = (x_buf[c, :, cols].astype(F32) + gain * normed).astype(BF16)
+        dout = og_buf[c, :, cols].astype(F32)
         ngrad_ref[0, h : h + 1, :] += jnp.sum(dout * normed, axis=0, keepdims=True)
         dn = dout * gain
         dz = rstd * (dn - row_mean(dn) - normed * row_mean(dn * normed))
@@ -175,15 +234,12 @@
         ls[c, h] = back[:width]
         v0s[c, h] = back[width:]
 
-    def retreat(c, h):
-        g = igrad_ref[0, h]
-        g2 = split(g)
-        put(gs, c, h, g2)
-        igrad_ref[0, h] = g - product(get(fs, c, h), g2, TN) + ls[c, h]
-
-    def gradients(c, h):
+    def retreat(c, h, g2):
+        igrad_ref[0, h] = igrad_ref[0, h] - product(get(fs, c, h), g2, TN) + ls[c, h]
+
+    def gradients(c, h, g2):
         cols = columns_of(h)
-        g2, kr2, w2, r2, dz2 = get(gs, c, h), get(krs, c, h), get(ws, c, h), get(rs, c, h), get(dzs, c, h)
+        kr2, w2, r2, dz2 = get(krs, c, h), get(ws, c, h), get(rs, c, h), get(dzs, c, h)
         v = v0s[c, h] + product(kr2, g2, NN)
         du = -product(get(ts, c, h), split(v), TN)
         both = stack(dz2, split(du), 0)
@@ -201,40 +257,66 @@
         drate = jnp.sum(dkr * k, axis=-1, keepdims=True) * rate_factor
         rgrad_ref[:, h : h + 1] += jnp.sum(drate, axis=0, keepdims=True)
         dlogit = drate * base * (1.0 - sig)
-        x = x_ref[c, :, cols]
+        x = x_buf[c, :, cols]
         ggrad_ref[0, h : h + 1, :] += jnp.sum(dlogit * x.astype(F32), axis=0, keepdims=True)
         packed = split(cat([dqk[:size], draw, -du], 1))
         vgrad_ref[0, h] += dot(cat([x, x], 0), cat(packed, 0), TN)
         views = view_buf[h]
         dx = dot(packed[0], views, NT) + dot(packed[1], views, NT)
-        dx = dx + og_ref[c, :, cols].astype(F32) + dlogit * gate_of(h)
-        dx_ref[c, :, cols] = dx.astype(BF16)
+        dx = dx + og_buf[c, :, cols].astype(F32) + dlogit * gate_of(h)
+        dx_buf[c, :, cols] = dx.astype(BF16)
 
     for ref in (vgrad_ref, ggrad_ref, rgrad_ref, ngrad_ref, igrad_ref):
         ref[...] = jnp.zeros_like(ref)
 
     all_heads = range(heads)
 
-    def forward(c, carry):
+    def prepare_step(step, carry):
+        c = partner(step)
+        arrived(x_buf, x_recv, c)
         for h in all_heads:
             prepare(c, h)
+        return carry
+
+    half = count // 2
+    lax.fori_loop(0, half, prepare_step, 0)
+    for step in range(1, count):
+        spread(og_ref, og_buf, og_send, og_recv, step).start()
+    lax.fori_loop(half, count, prepare_step, 0)
+
+    def forward(c, carry):
+        arrived(og_buf, og_recv, c)
+        starts = [split(init_buf[h]) for h in all_heads]
         for h in all_heads:
-            advance(c, h)
+            put(ws, c, h, starts[h])
+            advance(c, h, starts[h])
         for h in all_heads:
-            outputs(c, h)
+            outputs(c, h, starts[h])
+        collect(out_buf, next_ref, out_send, out_recv, c, after).start()
         return carry
 
     lax.fori_loop(0, count, forward, 0)
 
     def backward(step, carry):
         c = count - 1 - step
+        ends = [split(igrad_ref[0, h]) for h in all_heads]
         for h in all_heads:
-            retreat(c, h)
+            retreat(c, h, ends[h])
         for h in all_heads:
-            gradients(c, h)
+            gradients(c, h, ends[h])
+        collect(dx_buf, prev_ref, dx_send, dx_recv, c, before_me).start()
         return carry
 
     lax.fori_loop(0, count, backward, 0)
+
+    for step in range(1, count):
+        spread(x_ref, x_buf, x_send, x_recv, step).wait_send()
+        spread(og_ref, og_buf, og_send, og_recv, step).wait_send()
+    for c in range(count):
+        collect(out_buf, next_ref, out_send, out_recv, c, after).wait_send()
+        collect(dx_buf, prev_ref, dx_send, dx_recv, c, before_me).wait_send()
+        collected(next_ref, out_recv, c)
+        collected(prev_ref, dx_recv, c)
 
 
 def per_device(segment_input, views, gate_vec, base_rate, norm_gain, init_weight, out_grad):
@@ -244,59 +326,52 @@
     heads = total // count
     local = heads * width
 
-    def spread(value):
-        parts = value[0].reshape(size, count, local).swapaxes(0, 1)
-        return lax.all_to_all(parts, "ctx", 0, 0, tiled=True)
-
-    def collect(value, steps):
-        moved = lax.all_to_all(value, "ctx", 0, 0, tiled=True)
-        number = lax.axis_size("segment")
-        pairs = [(source, (source + steps) % number) for source in range(number)]
-        moved = lax.ppermute(moved, "segment", pairs)
-        return moved.swapaxes(0, 1).reshape(1, size, features)
-
     def shaped(shape, kind):
         return jax.ShapeDtypeStruct(shape, kind)
 
     vmem = pl.BlockSpec(memory_space=pltpu.VMEM)
     hbm = pl.BlockSpec(memory_space=pl.ANY)
 
+    chunks = pltpu.VMEM((count, size, local), BF16)
+
     def pairs(rows, columns):
         return pltpu.VMEM((count, heads, 2, rows, columns), BF16)
 
     def floats(rows, columns):
         return pltpu.VMEM((count, heads, rows, columns), F32)
 
-    result = pl.pallas_call(
-        functools.partial(kernel, count, heads, size, width),
+    return pl.pallas_call(
+        functools.partial(kernel, count, lax.axis_size("segment"), heads, size, width),
         out_shape=(
-            shaped((count, size, local), BF16),
+            shaped((1, size, features), BF16),
             shaped((1, heads, width, 3 * width), F32),
             shaped((1, heads, width), F32),
             shaped((1, heads), F32),
             shaped((1, heads, width), F32),
             shaped((1, heads, width, width), F32),
-            shaped((count, size, local), BF16),
+            shaped((1, size, features), BF16),
         ),
-        in_specs=[vmem, vmem, hbm, vmem, vmem, vmem, hbm],
-        out_specs=(vmem,) * 7,
+        in_specs=[hbm, hbm, hbm, vmem, vmem, vmem, hbm],
+        out_specs=(hbm,) + (vmem,) * 5 + (hbm,),
         scratch_shapes=[
             pltpu.VMEM((heads, width, 3 * width), BF16),
             pltpu.VMEM((heads, width, width), F32),
+            chunks, chunks, chunks, chunks,
             pairs(size, width), pairs(size, width), pairs(size, width), pairs(size, width), pairs(size, width),
             pairs(size, size), pairs(size, size), pairs(width, width),
-            pairs(size, width), pairs(size, width), pairs(width, width), pairs(width, width),
+            pairs(size, width), pairs(size, width), pairs(width, width),
             floats(size, width), floats(size, width), floats(size, width), floats(width, width),
             floats(size, width), floats(width, width),
             floats(size, 1), floats(size, 1),
             pltpu.SemaphoreType.DMA((2,)),
+            *[pltpu.SemaphoreType.DMA((count,))] * 8,
         ],
-        compiler_params=pltpu.CompilerParams(vmem_limit_bytes=56 * 1024 * 1024),
+        compiler_params=pltpu.CompilerParams(
+            vmem_limit_bytes=56 * 1024 * 1024, collective_id=0, has_side_effects=True
+        ),
     )(
-        spread(segment_input), spread(out_grad), views, gate_vec, base_rate, norm_gain, init_weight
+        segment_input, out_grad, views, gate_vec, base_rate, norm_gain, init_weight
     )
-    out, vgrad, ggrad, rgrad, ngrad, igrad, dx = result
-    return (collect(out, 1), vgrad, ggrad, rgrad, ngrad, igrad, collect(dx, -1))
 
 
 def solution(mesh):

time: 142 us -> 71.4 us (0.50)
  waiting for transfers between devices: 39.2 us -> 0 us
  blocking collectives: 37.2 us -> 0 us
  Pallas kernels: 45 us -> 63.7 us
  starting transfers between devices: 13.8 us -> 0 us
    all_to_all x2 -> x0, blocking collectives: 37.2 us -> none  [the longest x1 18.8 us: collect(): moved = lax.all_to_all(value, 'ctx', 0, 0, tiled=True)]
    all_to_all x2 -> x0, waiting for transfers between devices: 27.6 us -> none  [the longest x1 14.9 us: spread(): return lax.all_to_all(parts, 'ctx', 0, 0, tiled=True)]
    pallas_call x1, Pallas kernels: 45 us -> 63.7 us  [per_device(): pl.pallas_call(functools.partial(kernel, count, lax.axis_size('segment'),...]
    ppermute x2 -> x0, waiting for transfers between devices: 11.6 us -> none  [collect(): moved = lax.ppermute(moved, 'segment', pairs)]
    all_to_all x2 -> x0, starting transfers between devices: 9.82 us -> none  [the longest x1 6.33 us: spread(): return lax.all_to_all(parts, 'ctx', 0, 0, tiled=True)]
    ppermute x2 -> x0, starting transfers between devices: 3.99 us -> none  [collect(): moved = lax.ppermute(moved, 'segment', pairs)]
    unnamed x8 -> x17, local copies, waits for them, and re-layouts: 3.67 us -> 6.82 us
  transfers between devices with their start and end apart: 4 -> 0, of which waited for: 3 -> 0; matrix products, arithmetic and copies ran while one was open for 1% -> 0% of each run, Pallas kernels for 0% -> 0%
where the time goes in v1:
time: 71.4 us; the launch traced here: 71.2 us
  Pallas kernels  63.7 us (89%)
  local copies, waits for them, and re-layouts  6.82 us (10%)
    pallas_call x1, Pallas kernels, per_device(): pl.pallas_call(functools.partial(kernel, count, lax.axis_size('segment'),...  63.7 us
    unnamed x17, local copies, waits for them, and re-layouts  6.82 us

profile of v1, /device:TPU:0, one launch (start us, length us, event | category | flops | bytes accessed | tf_op | source)
XLA Modules:
  0.0 71.2 jit_solution(13562064684810679604)
XLA Ops:
  0.6 63.7 %shard_map.126 = (bf16[1,128,2048]{2,1,0:T(8,128)(2,1)}, f32[1,2,128,384]{3,2,1,0:T(8,128)}, f32[1,2,128]{2,1,0:T(2,128)}, f32[1,2]{1,0:T(1,128)}, f32[1,2,128]{...) custom-call(bf16[1,128,2048]{2,1,0:T(8,128)(2,1)} %x_ref.1, bf16[1,128,2048]{2,1,0:T(8,128)(2,1)} %og_ref.1, ...), custom_call_target="tpu_custom_call" | custom-call | tf_op jit(solution)/shard_map/pallas_call | solution.py:343
  64.3 0.0 copy-start.3
  64.4 0.0 copy-start.4
  64.4 0.0 copy-start.2
  64.4 0.0 copy-start.1
  64.4 0.0 copy-start
  64.4 1.9 %copy.21 = bf16[1,128,2048]{2,1,0:T(8,128)(2,1)} copy(bf16[1,128,2048]{2,1,0:T(8,128)(2,1)} %get-tuple-element.14) | data formatting | bytes 1048576
  66.3 1.8 %copy.22 = f32[1,2,128,384]{3,2,1,0:T(8,128)} copy(f32[1,2,128,384]{3,2,1,0:T(8,128)} %get-tuple-element.15) | data formatting | bytes 786432
  68.1 0.0 copy-done.3
  68.1 0.6 copy.23
  68.7 0.0 copy-done.4
  68.7 0.5 copy.24
  69.2 0.0 copy-done.2
  69.2 0.6 copy.25
  69.7 0.0 copy-done.1
  69.8 0.7 copy.26
  70.4 0.0 copy-done
  70.4 0.8 %copy.27 = bf16[1,128,2048]{2,1,0:T(8,128)(2,1)} copy(bf16[1,128,2048]{2,1,0:T(8,128)(2,1)S(1)} %copy-done) | data formatting | bytes 1048576
Async XLA Ops:
  64.3 3.8 %copy-start.3 = (f32[1,2,128]{2,1,0:T(2,128)S(1)}, f32[1,2,128]{2,1,0:T(2,128)}, u32[]{:S(2)}) copy-start(f32[1,2,128]{2,1,0:T(2,128)} %get-tuple-element.16) | copy-start | bytes 3076
  64.4 4.3 %copy-start.4 = (f32[1,2]{1,0:T(1,128)S(1)}, f32[1,2]{1,0:T(1,128)}, u32[]{:S(2)}) copy-start(f32[1,2]{1,0:T(1,128)} %get-tuple-element.17) | copy-start | bytes 28
  64.4 4.8 %copy-start.2 = (f32[1,2,128]{2,1,0:T(2,128)S(1)}, f32[1,2,128]{2,1,0:T(2,128)}, u32[]{:S(2)}) copy-start(f32[1,2,128]{2,1,0:T(2,128)} %get-tuple-element.18) | copy-start | bytes 3076
  64.4 5.4 %copy-start.1 = (f32[1,2,128,128]{3,2,1,0:T(8,128)S(1)}, f32[1,2,128,128]{3,2,1,0:T(8,128)}, u32[]{:S(2)}) copy-start(f32[1,2,128,128]{3,2,1,0:T(8,128)} %get-tuple-element.19) | copy-start | bytes 393220
  64.4 6.0 %copy-start = (bf16[1,128,2048]{2,1,0:T(8,128)(2,1)S(1)}, bf16[1,128,2048]{2,1,0:T(8,128)(2,1)}, u32[]{:S(2)}) copy-start(bf16[1,128,2048]{2,1,0:T(8,128)(2,1)} %get-tuple-element.20) | copy-start | bytes 1572868

commit v2 on v1

--- a/solution.py
+++ b/solution.py
@@ -47,35 +47,44 @@
     return jnp.mean(value, axis=-1, keepdims=True)
 
 
-def positions(size):
+def fill_masks(ref, size):
     rows = lax.broadcasted_iota(jnp.int32, (size, size), 0)
     columns = lax.broadcasted_iota(jnp.int32, (size, size), 1)
-    return rows, columns
-
-
-def block_inverse(strict, size):
-    rows, columns = positions(size)
-    width = MB
-    eye = jnp.where(rows == columns, 1.0, 0.0).astype(F32)
-    inverse = eye
-    while width < size:
-        same = (rows // (2 * width)) == (columns // (2 * width))
-        below = (rows // width) > (columns // width)
-        corner = jnp.where(same & below, strict, 0.0)
-        if width == MB:
-            inverse = eye - corner
-        else:
-            pair = split(inverse)
-            inverse = inverse - product(split(product(pair, split(corner), NN)), pair, NN)
-        width *= 2
-    return inverse
+    chosen = [rows >= columns, (rows // MB) > (columns // MB), rows == columns]
+    block = MB
+    while block < size:
+        same = (rows // (2 * block)) == (columns // (2 * block))
+        chosen.append(same & ((rows // block) > (columns // block)))
+        block *= 2
+    for index, mask in enumerate(chosen):
+        ref[index] = jnp.where(mask, 1.0, 0.0).astype(F32)
+
+
+def levels_of(size):
+    levels, block = 0, MB
+    while block < size:
+        levels, block = levels + 1, 2 * block
+    return levels
+
+
+def together(streams):
+    streams = list(streams)
+    while streams:
+        alive = []
+        for stream in streams:
+            try:
+                next(stream)
+                alive.append(stream)
+            except StopIteration:
+                pass
+        streams = alive
 
 
 def kernel(
     count, sections, heads, size, width,
     x_ref, og_ref, views_ref, gate_ref, rate_ref, gain_ref, init_ref,
     next_ref, vgrad_ref, ggrad_ref, rgrad_ref, ngrad_ref, igrad_ref, prev_ref,
-    view_buf, init_buf, x_buf, og_buf, out_buf, dx_buf,
+    view_buf, init_buf, x_buf, og_buf, out_buf, dx_buf, masks,
     qs, ks, krs, qes, as_, ss, ts, fs, rs, dzs, ws,
     kf, bs, sbs, os_, v0s, ls, invs, sigs,
     load_sem, x_send, x_recv, og_send, og_recv, out_send, out_recv, dx_send, dx_recv,
@@ -149,6 +158,8 @@
     for load in loads[:2]:
         load.wait()
     scale = 1.0 / (MB * width)
+    levels = levels_of(size)
+    fill_masks(masks, size)
 
     def columns_of(h):
         return slice(h * width, (h + 1) * width)
@@ -170,13 +181,10 @@
     def get(ref, c, h):
         return ref[c, h, 0], ref[c, h, 1]
 
-    def masks():
-        rows, columns = positions(size)
-        return rows >= columns, (rows // MB) > (columns // MB)
-
     def prepare(c, h):
         x = x_buf[c, :, columns_of(h)]
         packed = dot(x, view_buf[h], NN)
+        yield
         q = packed[:, :width]
         raw = packed[:, width : 2 * width]
         inv = lax.rsqrt(row_mean(raw * raw) + 1e-06)
@@ -186,15 +194,26 @@
         sig = jax.nn.sigmoid(logit)
         kr = k * (base_of(h) * sig * scale)
         k2, q2, kr2 = split(k), split(q), split(kr)
-        causal, before = masks()
+        y2 = split(y)
+        yield
         grams = product(stack(k2, q2, 0), kr2, NT)
-        inverse = block_inverse(jnp.where(before, grams[:size], 0.0), size)
-        scores = split(jnp.where(causal, grams[size:], 0.0))
+        yield
+        scores = split(masks[0] * grams[size:])
+        strict = grams[:size]
+        inverse = masks[2] - masks[3] * strict if levels else masks[2]
         t2 = split(inverse)
-        ab = product(t2, stack(k2, split(y), 1), NN)
+        for level in range(1, levels):
+            half_way = product(t2, split(masks[3 + level] * strict), NN)
+            yield
+            inverse = inverse - product(split(half_way), t2, NN)
+            t2 = split(inverse)
+            yield
+        ab = product(t2, stack(k2, y2, 1), NN)
+        yield
         ab2 = split(ab)
         sab = product(scores, ab2, NN)
         fo = product(kr2, ab2, TN)
+        yield
         put(qs, c, h, q2)
         put(ks, c, h, k2)
         put(krs, c, h, kr2)
@@ -210,16 +229,15 @@
         invs[c, h] = inv
         sigs[c, h] = sig
 
-    def advance(c, h, w2):
-        init_buf[h] = init_buf[h] - product(get(fs, c, h), w2, NN) + os_[c, h]
-
     def outputs(c, h, w2):
         cols = columns_of(h)
         qe = get(qes, c, h)
         moved = product(stack(qe, get(as_, c, h), 0), w2, NN)
+        yield
         z = moved[:size] + sbs[c, h]
         put(rs, c, h, split(moved[size:] - bs[c, h]))
         centred = z - row_mean(z)
+        yield
         rstd = lax.rsqrt(row_mean(centred * centred) + 1e-05)
         normed = centred * rstd
         gain = gain_of(h)
@@ -230,26 +248,27 @@
         dz = rstd * (dn - row_mean(dn) - normed * row_mean(dn * normed))
         dz2 = split(dz)
         put(dzs, c, h, dz2)
+        yield
         back = product(stack(qe, get(ss, c, h), 1), dz2, TN)
+        yield
         ls[c, h] = back[:width]
         v0s[c, h] = back[width:]
-
-    def retreat(c, h, g2):
-        igrad_ref[0, h] = igrad_ref[0, h] - product(get(fs, c, h), g2, TN) + ls[c, h]
 
     def gradients(c, h, g2):
         cols = columns_of(h)
         kr2, w2, r2, dz2 = get(krs, c, h), get(ws, c, h), get(rs, c, h), get(dzs, c, h)
         v = v0s[c, h] + product(kr2, g2, NN)
+        yield
         du = -product(get(ts, c, h), split(v), TN)
+        yield
         both = stack(dz2, split(du), 0)
-        causal, before = masks()
         inner = product(both, r2, NT)
-        dscores = jnp.where(causal, -inner[:size], 0.0)
-        dstrict = jnp.where(before, -inner[size:], 0.0)
-        d2 = stack(split(dscores), split(dstrict), 0)
+        yield
+        d2 = stack(split(-masks[0] * inner[:size]), split(-masks[1] * inner[size:]), 0)
         dqk = product(both, w2, NT) + product(d2, kr2, NN)
+        yield
         dkr = product(d2, stack(get(qs, c, h), get(ks, c, h), 0), TN) - product(r2, g2, NT)
+        yield
         sig, inv, k, base = sigs[c, h], invs[c, h], kf[c, h], base_of(h)
         rate_factor = sig * scale
         dk = dqk[size:] + (base * rate_factor) * dkr + du
@@ -260,6 +279,7 @@
         x = x_buf[c, :, cols]
         ggrad_ref[0, h : h + 1, :] += jnp.sum(dlogit * x.astype(F32), axis=0, keepdims=True)
         packed = split(cat([dqk[:size], draw, -du], 1))
+        yield
         vgrad_ref[0, h] += dot(cat([x, x], 0), cat(packed, 0), TN)
         views = view_buf[h]
         dx = dot(packed[0], views, NT) + dot(packed[1], views, NT)
@@ -271,43 +291,77 @@
 
     all_heads = range(heads)
 
+    pairing = 2 if count % 4 == 0 else 1
+    by = range(pairing)
+
     def prepare_step(step, carry):
-        c = partner(step)
-        arrived(x_buf, x_recv, c)
-        for h in all_heads:
-            prepare(c, h)
+        chunks = [partner(step * pairing + i) for i in by]
+        for c in chunks:
+            arrived(x_buf, x_recv, c)
+        together(prepare(c, h) for c in chunks for h in all_heads)
         return carry
 
-    half = count // 2
+    rounds = count // pairing
+    half = rounds // 2
     lax.fori_loop(0, half, prepare_step, 0)
     for step in range(1, count):
         spread(og_ref, og_buf, og_send, og_recv, step).start()
-    lax.fori_loop(half, count, prepare_step, 0)
-
-    def forward(c, carry):
-        arrived(og_buf, og_recv, c)
-        starts = [split(init_buf[h]) for h in all_heads]
+    lax.fori_loop(half, rounds, prepare_step, 0)
+
+    def forward_stream(c, h, w, ends):
+        w2 = split(w)
+        put(ws, c, h, w2)
+        ends[h] = w - product(get(fs, c, h), w2, NN) + os_[c, h]
+        yield
+        yield from outputs(c, h, w2)
+
+    def forward(step, carry):
+        chunks = [step * pairing + i for i in by]
+        for c in chunks:
+            arrived(og_buf, og_recv, c)
+        now = {h: init_buf[h] for h in all_heads}
+        streams = []
+        for c in chunks:
+            ends = {}
+            fresh = [forward_stream(c, h, now[h], ends) for h in all_heads]
+            for stream in fresh:
+                next(stream)
+            streams += fresh
+            now = ends
         for h in all_heads:
-            put(ws, c, h, starts[h])
-            advance(c, h, starts[h])
+            init_buf[h] = now[h]
+        together(streams)
+        for c in chunks:
+            collect(out_buf, next_ref, out_send, out_recv, c, after).start()
+        return carry
+
+    lax.fori_loop(0, rounds, forward, 0)
+
+    def backward_stream(c, h, g, starts):
+        g2 = split(g)
+        starts[h] = g - product(get(fs, c, h), g2, TN) + ls[c, h]
+        yield
+        yield from gradients(c, h, g2)
+
+    def backward(step, carry):
+        chunks = [count - 1 - (step * pairing + i) for i in by]
+        now = {h: igrad_ref[0, h] for h in all_heads}
+        streams = []
+        for c in chunks:
+            starts = {}
+            fresh = [backward_stream(c, h, now[h], starts) for h in all_heads]
+            for stream in fresh:
+                next(stream)
+            streams += fresh
+            now = starts
         for h in all_heads:
-            outputs(c, h, starts[h])
-        collect(out_buf, next_ref, out_send, out_recv, c, after).start()
+            igrad_ref[0, h] = now[h]
+        together(streams)
+        for c in chunks:
+            collect(dx_buf, prev_ref, dx_send, dx_recv, c, before_me).start()
         return carry
 
-    lax.fori_loop(0, count, forward, 0)
-
-    def backward(step, carry):
-        c = count - 1 - step
-        ends = [split(igrad_ref[0, h]) for h in all_heads]
-        for h in all_heads:
-            retreat(c, h, ends[h])
-        for h in all_heads:
-            gradients(c, h, ends[h])
-        collect(dx_buf, prev_ref, dx_send, dx_recv, c, before_me).start()
-        return carry
-
-    lax.fori_loop(0, count, backward, 0)
+    lax.fori_loop(0, rounds, backward, 0)
 
     for step in range(1, count):
         spread(x_ref, x_buf, x_send, x_recv, step).wait_send()
@@ -319,6 +373,15 @@
         collected(prev_ref, dx_recv, c)
 
 
+def hand_over(*refs):
+    number = (len(refs) - 1) // 2
+    copies = [pltpu.make_async_copy(refs[i], refs[number + i], refs[-1].at[i]) for i in range(number)]
+    for copy in copies:
+        copy.start()
+    for copy in copies:
+        copy.wait()
+
+
 def per_device(segment_input, views, gate_vec, base_rate, norm_gain, init_weight, out_grad):
     count = lax.axis_size("ctx")
     size, features = segment_input.shape[1:]
@@ -340,7 +403,7 @@
     def floats(rows, columns):
         return pltpu.VMEM((count, heads, rows, columns), F32)
 
-    return pl.pallas_call(
+    results = pl.pallas_call(
         functools.partial(kernel, count, lax.axis_size("segment"), heads, size, width),
         out_shape=(
             shaped((1, size, features), BF16),
@@ -357,6 +420,7 @@
             pltpu.VMEM((heads, width, 3 * width), BF16),
             pltpu.VMEM((heads, width, width), F32),
             chunks, chunks, chunks, chunks,
+            pltpu.VMEM((3 + levels_of(size), size, size), F32),
             pairs(size, width), pairs(size, width), pairs(size, width), pairs(size, width), pairs(size, width),
             pairs(size, size), pairs(size, size), pairs(width, width),
             pairs(size, width), pairs(size, width), pairs(width, width),
@@ -372,6 +436,13 @@
     )(
         segment_input, out_grad, views, gate_vec, base_rate, norm_gain, init_weight
     )
+    return pl.pallas_call(
+        hand_over,
+        out_shape=tuple(shaped(value.shape, value.dtype) for value in results),
+        in_specs=[hbm] * len(results),
+        out_specs=(vmem,) * len(results),
+        scratch_shapes=[pltpu.SemaphoreType.DMA((len(results),))],
+    )(*results)
 
 
 def solution(mesh):

time: 71.4 us -> 61 us (0.85)
  local copies, waits for them, and re-layouts: 6.82 us -> 0 us
  Pallas kernels: 63.7 us -> 60.1 us
    unnamed x17 -> x0, local copies, waits for them, and re-layouts: 6.82 us -> none
    pallas_call x1, Pallas kernels: 63.7 us -> 57.5 us  [per_device(): pl.pallas_call(functools.partial(kernel, count, lax.axis_size('segment'),...]
    pallas_call x0 -> x1, Pallas kernels: none -> 2.58 us  [per_device(): pl.pallas_call(hand_over, out_shape=tuple((shaped(value.shape, value.dtyp...]
where the time goes in v2:
time: 61 us; the launch traced here: 60.8 us
  Pallas kernels  60.1 us (99%)
  between operations  0.64 us (1%)
    pallas_call x1, Pallas kernels, per_device(): pl.pallas_call(functools.partial(kernel, count, lax.axis_size('segment'),...  57.5 us
    pallas_call x1, Pallas kernels, per_device(): pl.pallas_call(hand_over, out_shape=tuple((shaped(value.shape, value.dtyp...  2.58 us

profile of v2, /device:TPU:0, one launch (start us, length us, event | category | flops | bytes accessed | tf_op | source)
XLA Modules:
  0.0 60.8 jit_solution(8943418227370853508)
XLA Ops:
  0.6 57.5 %shard_map.126 = (bf16[1,128,2048]{2,1,0:T(8,128)(2,1)}, f32[1,2,128,384]{3,2,1,0:T(8,128)}, f32[1,2,128]{2,1,0:T(2,128)}, f32[1,2]{1,0:T(1,128)}, f32[1,2,128]{...) custom-call(bf16[1,128,2048]{2,1,0:T(8,128)(2,1)} %x_ref.1, bf16[1,128,2048]{2,1,0:T(8,128)(2,1)} %og_ref.1, ...), custom_call_target="tpu_custom_call" | custom-call | tf_op jit(solution)/shard_map/pallas_call | solution.py:406
  58.2 2.6 %shard_map.127 = (bf16[1,128,2048]{2,1,0:T(8,128)(2,1)}, f32[1,2,128,384]{3,2,1,0:T(8,128)}, f32[1,2,128]{2,1,0:T(2,128)}, f32[1,2]{1,0:T(1,128)}, f32[1,2,128]{...) custom-call(bf16[1,128,2048]{2,1,0:T(8,128)(2,1)} %get-tuple-element.14.refs_0_, ...), custom_call_target="tpu_custom_call" | custom-call | tf_op jit(solution)/shard_map/pallas_call | solution.py:439

commit v3 on v2

--- a/solution.py
+++ b/solution.py
@@ -85,8 +85,8 @@
     x_ref, og_ref, views_ref, gate_ref, rate_ref, gain_ref, init_ref,
     next_ref, vgrad_ref, ggrad_ref, rgrad_ref, ngrad_ref, igrad_ref, prev_ref,
     view_buf, init_buf, x_buf, og_buf, out_buf, dx_buf, masks,
-    qs, ks, krs, qes, as_, ss, ts, fs, rs, dzs, ws,
-    kf, bs, sbs, os_, v0s, ls, invs, sigs,
+    qs, ks, krs, qes, as_, ss, ts, fs, rs, dzs, ws, gs,
+    kf, bs, sbs, os_, v0s, ls, ns, invs, sigs, rstds,
     load_sem, x_send, x_recv, og_send, og_recv, out_send, out_recv, dx_send, dx_recv,
 ):
     me = lax.axis_index("ctx")
@@ -105,6 +105,11 @@
             bit *= 2
         return total
 
+    def turn(step):
+        if count % 2:
+            return partner(step)
+        return partner((step % 2) * (count // 2) + step // 2)
+
     def own_columns(owner):
         return pl.ds(pl.multiple_of(owner * local, local), local)
 
@@ -126,7 +131,7 @@
     pl.semaphore_wait(barrier, 3 * count - 1)
 
     def spread(source, target, send, receive, step):
-        owner = partner(step)
+        owner = turn(step)
         return pltpu.make_async_remote_copy(
             src_ref=source.at[0, :, own_columns(owner)],
             dst_ref=target.at[me],
@@ -229,10 +234,9 @@
         invs[c, h] = inv
         sigs[c, h] = sig
 
-    def outputs(c, h, w2):
+    def emit(c, h):
         cols = columns_of(h)
-        qe = get(qes, c, h)
-        moved = product(stack(qe, get(as_, c, h), 0), w2, NN)
+        moved = product(stack(get(qes, c, h), get(as_, c, h), 0), get(ws, c, h), NN)
         yield
         z = moved[:size] + sbs[c, h]
         put(rs, c, h, split(moved[size:] - bs[c, h]))
@@ -240,22 +244,28 @@
         yield
         rstd = lax.rsqrt(row_mean(centred * centred) + 1e-05)
         normed = centred * rstd
-        gain = gain_of(h)
-        out_buf[c, :, cols] = (x_buf[c, :, cols].astype(F32) + gain * normed).astype(BF16)
-        dout = og_buf[c, :, cols].astype(F32)
+        out_buf[c, :, cols] = (x_buf[c, :, cols].astype(F32) + gain_of(h) * normed).astype(BF16)
+        ns[c, h] = normed
+        rstds[c, h] = rstd
+        yield
+
+    def receive_grad(c, h):
+        dout = og_buf[c, :, columns_of(h)].astype(F32)
+        normed = ns[c, h]
         ngrad_ref[0, h : h + 1, :] += jnp.sum(dout * normed, axis=0, keepdims=True)
-        dn = dout * gain
-        dz = rstd * (dn - row_mean(dn) - normed * row_mean(dn * normed))
+        dn = dout * gain_of(h)
+        dz = rstds[c, h] * (dn - row_mean(dn) - normed * row_mean(dn * normed))
         dz2 = split(dz)
         put(dzs, c, h, dz2)
         yield
-        back = product(stack(qe, get(ss, c, h), 1), dz2, TN)
-        yield
+        back = product(stack(get(qes, c, h), get(ss, c, h), 1), dz2, TN)
         ls[c, h] = back[:width]
         v0s[c, h] = back[width:]
-
-    def gradients(c, h, g2):
+        yield
+
+    def gradients(c, h):
         cols = columns_of(h)
+        g2 = get(gs, c, h)
         kr2, w2, r2, dz2 = get(krs, c, h), get(ws, c, h), get(rs, c, h), get(dzs, c, h)
         v = v0s[c, h] + product(kr2, g2, NN)
         yield
@@ -295,7 +305,7 @@
     by = range(pairing)
 
     def prepare_step(step, carry):
-        chunks = [partner(step * pairing + i) for i in by]
+        chunks = [turn(step * pairing + i) for i in by]
         for c in chunks:
             arrived(x_buf, x_recv, c)
         together(prepare(c, h) for c in chunks for h in all_heads)
@@ -308,60 +318,53 @@
         spread(og_ref, og_buf, og_send, og_recv, step).start()
     lax.fori_loop(half, rounds, prepare_step, 0)
 
-    def forward_stream(c, h, w, ends):
-        w2 = split(w)
-        put(ws, c, h, w2)
-        ends[h] = w - product(get(fs, c, h), w2, NN) + os_[c, h]
-        yield
-        yield from outputs(c, h, w2)
-
-    def forward(step, carry):
-        chunks = [step * pairing + i for i in by]
+    def advance(c, carry):
+        for h in all_heads:
+            w = init_buf[h]
+            w2 = split(w)
+            put(ws, c, h, w2)
+            init_buf[h] = w - product(get(fs, c, h), w2, NN) + os_[c, h]
+        return carry
+
+    lax.fori_loop(0, count, advance, 0)
+
+    def emit_step(step, carry):
+        chunks = [turn(count - 1 - (step * pairing + i)) for i in by]
+        together(emit(c, h) for c in chunks for h in all_heads)
+        for c in chunks:
+            collect(out_buf, next_ref, out_send, out_recv, c, after).start()
+        return carry
+
+    lax.fori_loop(0, rounds, emit_step, 0)
+
+    def receive_step(step, carry):
+        chunks = [turn(step * pairing + i) for i in by]
         for c in chunks:
             arrived(og_buf, og_recv, c)
-        now = {h: init_buf[h] for h in all_heads}
-        streams = []
-        for c in chunks:
-            ends = {}
-            fresh = [forward_stream(c, h, now[h], ends) for h in all_heads]
-            for stream in fresh:
-                next(stream)
-            streams += fresh
-            now = ends
+        together(receive_grad(c, h) for c in chunks for h in all_heads)
+        return carry
+
+    lax.fori_loop(0, rounds, receive_step, 0)
+
+    def retreat(step, carry):
+        c = count - 1 - step
         for h in all_heads:
-            init_buf[h] = now[h]
-        together(streams)
-        for c in chunks:
-            collect(out_buf, next_ref, out_send, out_recv, c, after).start()
-        return carry
-
-    lax.fori_loop(0, rounds, forward, 0)
-
-    def backward_stream(c, h, g, starts):
-        g2 = split(g)
-        starts[h] = g - product(get(fs, c, h), g2, TN) + ls[c, h]
-        yield
-        yield from gradients(c, h, g2)
-
-    def backward(step, carry):
-        chunks = [count - 1 - (step * pairing + i) for i in by]
-        now = {h: igrad_ref[0, h] for h in all_heads}
-        streams = []
-        for c in chunks:
-            starts = {}
-            fresh = [backward_stream(c, h, now[h], starts) for h in all_heads]
-            for stream in fresh:
-                next(stream)
-            streams += fresh
-            now = starts
-        for h in all_heads:
-            igrad_ref[0, h] = now[h]
-        together(streams)
+            g = igrad_ref[0, h]
+            g2 = split(g)
+            put(gs, c, h, g2)
+            igrad_ref[0, h] = g - product(get(fs, c, h), g2, TN) + ls[c, h]
+        return carry
+
+    lax.fori_loop(0, count, retreat, 0)
+
+    def gradient_step(step, carry):
+        chunks = [turn(count - 1 - (step * pairing + i)) for i in by]
+        together(gradients(c, h) for c in chunks for h in all_heads)
         for c in chunks:
             collect(dx_buf, prev_ref, dx_send, dx_recv, c, before_me).start()
         return carry
 
-    lax.fori_loop(0, rounds, backward, 0)
+    lax.fori_loop(0, rounds, gradient_step, 0)
 
     for step in range(1, count):
         spread(x_ref, x_buf, x_send, x_recv, step).wait_send()
@@ -423,10 +426,10 @@
             pltpu.VMEM((3 + levels_of(size), size, size), F32),
             pairs(size, width), pairs(size, width), pairs(size, width), pairs(size, width), pairs(size, width),
             pairs(size, size), pairs(size, size), pairs(width, width),
-            pairs(size, width), pairs(size, width), pairs(width, width),
+            pairs(size, width), pairs(size, width), pairs(width, width), pairs(width, width),
             floats(size, width), floats(size, width), floats(size, width), floats(width, width),
-            floats(size, width), floats(width, width),
-            floats(size, 1), floats(size, 1),
+            floats(size, width), floats(width, width), floats(size, width),
+            floats(size, 1), floats(size, 1), floats(size, 1),
             pltpu.SemaphoreType.DMA((2,)),
             *[pltpu.SemaphoreType.DMA((count,))] * 8,
         ],

time: 61 us -> 60.1 us (0.985)
  Pallas kernels: 60.1 us -> 59.2 us
    pallas_call x1, Pallas kernels: 57.5 us -> 56.6 us  [per_device(): pl.pallas_call(functools.partial(kernel, count, lax.axis_size('segment'),...]
where the time goes in v3:
time: 60.1 us; the launch traced here: 59.8 us
  Pallas kernels  59.2 us (99%)
  between operations  0.64 us (1%)
    pallas_call x1, Pallas kernels, per_device(): pl.pallas_call(functools.partial(kernel, count, lax.axis_size('segment'),...  56.6 us
    pallas_call x1, Pallas kernels, per_device(): pl.pallas_call(hand_over, out_shape=tuple((shaped(value.shape, value.dtyp...  2.58 us

profile of v3, /device:TPU:0, one launch (start us, length us, event | category | flops | bytes accessed | tf_op | source)
XLA Modules:
  0.0 59.8 jit_solution(263252715618380027)
XLA Ops:
  0.6 56.6 %shard_map.126 = (bf16[1,128,2048]{2,1,0:T(8,128)(2,1)}, f32[1,2,128,384]{3,2,1,0:T(8,128)}, f32[1,2,128]{2,1,0:T(2,128)}, f32[1,2]{1,0:T(1,128)}, f32[1,2,128]{...) custom-call(bf16[1,128,2048]{2,1,0:T(8,128)(2,1)} %x_ref.1, bf16[1,128,2048]{2,1,0:T(8,128)(2,1)} %og_ref.1, ...), custom_call_target="tpu_custom_call" | custom-call | tf_op jit(solution)/shard_map/pallas_call | solution.py:409
  57.2 2.6 %shard_map.127 = (bf16[1,128,2048]{2,1,0:T(8,128)(2,1)}, f32[1,2,128,384]{3,2,1,0:T(8,128)}, f32[1,2,128]{2,1,0:T(2,128)}, f32[1,2]{1,0:T(1,128)}, f32[1,2,128]{...) custom-call(bf16[1,128,2048]{2,1,0:T(8,128)(2,1)} %get-tuple-element.14.refs_0_, ...), custom_call_target="tpu_custom_call" | custom-call | tf_op jit(solution)/shard_map/pallas_call | solution.py:442
